TPU v7x, 128 devices: a whole 4x4x4 slice. The times are simulated.
128 devices in a mesh: blk: 32 (over z, x_lo, y), grp: 4 (over x_hi, core).
Axes of the slice: x: 4 (x_hi: 2, x_lo: 2; x = x_hi * 2 + x_lo), y: 4, z: 4, core: 2. Of those that a mesh axis runs over, the one named last changes fastest.
Arguments:
- acts: bfloat16 [1, 512, 256, 4096], P(None, 'blk', 'grp'), may hold values from -6 to 6
- out_grads: bfloat16 [1, 512, 256, 4096], P(None, 'blk', 'grp'), may hold values from -6 to 6
- proj_in: bfloat16 [1, 4096, 64], replicated, may hold values from -0.09375 to 0.09375
- proj_out: bfloat16 [1, 4096, 64], replicated, may hold values from -0.09375 to 0.09375
- lengths: int32 [512], P('blk'), may hold values from 1 to 256
- queries: bfloat16 [2048, 4096], P('blk'), may hold values from -0.09375 to 0.09375
Outputs:
- scores: float32 [512, 2048], P(('blk', 'grp'))
All inputs are finite; a program needn't handle non-finite values.
Results may differ from a plain program's by a relative error of at most 0.0049.
Values may be sent and summed in bfloat16 or wider, within the bound.
A program may use at most 128 MiB of HBM per device.

v0:
```python
import jax
import jax.numpy as jnp
from jax import lax
from jax.sharding import PartitionSpec as P


def project(rows, matrix):
    return jnp.einsum("lctd,ldr->lctr", rows, matrix, preferred_element_type=jnp.float32).astype(
        jnp.bfloat16
    )


def outer_sums(grad_side, input_side, lens):
    positions = jnp.arange(grad_side.shape[2], dtype=jnp.int32)
    masked = (positions[None, :] < lens[:, None]).astype(jnp.bfloat16)
    grad_masked = grad_side * masked[None, :, :, None]
    block = jnp.einsum(
        "lcta,lctb->clab", grad_masked, input_side, preferred_element_type=jnp.float32
    )
    return block.reshape(block.shape[0], -1)


def on_device(acts, out_grads, proj_in, proj_out, lengths, queries):
    group = lax.axis_index("grp")
    groups = lax.axis_size("grp")
    cand_blk = acts.shape[1]
    owned = cand_blk // groups
    stacked = jnp.concatenate([project(out_grads, proj_out), project(acts, proj_in)], axis=3)
    stacked = lax.all_to_all(stacked, "grp", split_axis=1, concat_axis=2, tiled=True)
    width = proj_in.shape[2]
    own_lens = lax.dynamic_slice_in_dim(lengths, group * owned, owned)
    grads = outer_sums(stacked[..., :width], stacked[..., width:], own_lens)
    scale = lax.rsqrt(jnp.mean(grads * grads, axis=1, keepdims=True) + 1e-06)
    unit = (grads * scale).astype(jnp.bfloat16)
    return lax.dot_general(
        unit,
        lax.all_gather(queries, "blk", axis=0, tiled=True),
        (((1,), (1,)), ((), ())),
        preferred_element_type=jnp.float32,
    )


def solution(mesh):
    in_specs = (
        P(None, "blk", "grp", None),
        P(None, "blk", "grp", None),
        P(),
        P(),
        P("blk"),
        P("blk", None),
    )
    out_specs = P(("blk", "grp"), None)
    return jax.shard_map(
        on_device, mesh=mesh, in_specs=in_specs, out_specs=out_specs, check_vma=False
    )
```

profile of v0, /device:TPU:0, one launch (start us, length us, event | category | flops | bytes accessed | tf_op | source)
XLA Modules:
  0.0 225.3 jit_solution(2176710123652143649)
XLA Ops:
  6.5 0.0 copy-start
  6.5 0.0 copy-start.2
  6.5 0.0 all-gather.2.cloned.1.call-start
  6.5 0.7 all-gather.2.cloned.1.call-update
  7.3 0.3 copy-done
  7.6 0.0 copy-start.1
  7.6 5.8 %fusion.10 = bf16[1,16,64,64]{3,2,1,0:T(8,128)(2,1)S(1)} fusion(bf16[1,16,64,4096]{3,2,1,0:T(8,128)(2,1)} %param.6, bf16[1,4096,64]{1,2,0:T(8,128)(2,1)S(1)} %copy-done), kind=kOutput, calls=%fused_computation.6 | convolution fusion | flops 536936448 | bytes 9043968 | tf_op jit(solution)/shard_map/lctd,ldr->lctr/dot_general | solution.py:8
  13.4 0.0 copy-done.2
  13.4 0.0 copy-done.1
  13.5 0.0 copy-start.3
  13.5 2.4 %fusion.13 = bf16[1,16,64,64]{3,2,1,0:T(8,128)(2,1)S(1)} fusion(bf16[1,16,64,4096]{3,2,1,0:T(8,128)(2,1)S(1)} %copy-done.1, bf16[1,4096,64]{1,2,0:T(8,128)(2,1)S(1)} %copy-done.2), kind=kOutput, calls=%fused_computation.7 | convolution fusion | flops 536936448 | bytes 9043968 | tf_op jit(solution)/shard_map/lctd,ldr->lctr/dot_general | solution.py:8
  15.8 0.9 maximum_bitcast_fusion
  16.7 4.4 %all-to-all-start = ((bf16[1,16,64,128]{3,2,0,1:T(8,128)(2,1)}), bf16[1,16,64,128]{3,2,0,1:T(8,128)(2,1)S(1)}, u32[]{:S(2)}, u32[]{:S(2)}) async-start(bf16[1,16,64,128]{3,2,0,1:T(8,128)(2,1)} %maximum_bitcast_fusion), calls=%async_computation | async-start | bytes 524288 | tf_op jit(solution)/shard_map/all_to_all | solution.py:29
  21.0 0.0 copy-done.3
  21.0 0.1 dynamic_slice.3
  21.1 0.1 fusion.24
  21.2 10.5 %all-to-all-done = bf16[1,16,64,128]{3,2,0,1:T(8,128)(2,1)S(1)} async-done(((bf16[1,16,64,128]{3,2,0,1:T(8,128)(2,1)}), bf16[1,16,64,128]{3,2,0,1:T(8,128)(2,1)S(1)}, u32[]{:S(2)}, u32[]{:S(2)}) %all-to-all-start) | async-done | bytes 262176 | tf_op jit(solution)/shard_map/all_to_all | solution.py:29
  31.7 0.6 multiply_reduce_fusion
  32.3 0.1 reshape.65
  32.4 175.2 %all-gather.2.cloned.1.call-done = bf16[2048,4096]{1,0:T(8,128)(2,1)} async-done(((bf16[64,4096]{1,0:T(8,128)(2,1)}), bf16[2048,4096]{1,0:T(8,128)(2,1)}) %all-gather.2.cloned.1.call-update) | async-done | bytes 16777232 | tf_op jit(solution)/shard_map/all_gather | solution.py:37
  207.6 10.8 %fusion.22 = f32[4,2048]{1,0:T(4,128)} fusion(bf16[2048,4096]{1,0:T(8,128)(2,1)} %all-gather.2.cloned.1.call-done, f32[4,4096]{1,0:T(4,128)S(1)} %reshape.65, f32[4]{0:T(128)S(1)} %add_rsqrt_fusion), kind=kOutput, calls=%fused_computation.18 | convolution fusion | flops 67141632 | bytes 16875536 | tf_op jit(solution)/shard_map/dot_general | solution.py:35
  (2 shorter events, 0.0 us)
Async XLA Ops:
  6.5 1.0 copy-start
  6.5 6.9 %copy-start.2 = (bf16[1,4096,64]{1,2,0:T(8,128)(2,1)S(1)}, bf16[1,4096,64]{1,2,0:T(8,128)(2,1)}, u32[]{:S(2)}) copy-start(bf16[1,4096,64]{1,2,0:T(8,128)(2,1)} %param.9) | copy-start | bytes 1572868
  6.5 201.1 %all-gather.2.cloned.1.call-start = ((), (), s32[]{:S(2)}) async-start(), calls=%async_computation.1 | async-start | bytes 17301504 | tf_op jit(solution)/shard_map/all_gather | solution.py:37
  7.6 5.9 %copy-start.1 = (bf16[1,16,64,4096]{3,2,1,0:T(8,128)(2,1)S(1)}, bf16[1,16,64,4096]{3,2,1,0:T(8,128)(2,1)}, u32[]{:S(2)}) copy-start(bf16[1,16,64,4096]{3,2,1,0:T(8,128)(2,1)} %param.7) | copy-start | bytes 25165828
  13.5 7.6 %copy-start.3 = (s32[16]{0:T(128)S(1)}, s32[16]{0:T(128)}, u32[]{:S(2)}) copy-start(s32[16]{0:T(128)} %param.10) | copy-start | bytes 196
  16.7 15.0 %all-to-all-start = ((bf16[1,16,64,128]{3,2,0,1:T(8,128)(2,1)}), bf16[1,16,64,128]{3,2,0,1:T(8,128)(2,1)S(1)}, u32[]{:S(2)}, u32[]{:S(2)}) async-start(bf16[1,16,64,128]{3,2,0,1:T(8,128)(2,1)} %maximum_bitcast_fusion), calls=%async_computation | async-start | bytes 524288 | tf_op jit(solution)/shard_map/all_to_all | solution.py:29
Sparse Core Ops, SparseCore 0:
  9.0 198.5 all-gather.1
where the time goes:
time: 226 us; the launch traced here: 225 us
  waiting for transfers between devices  186 us (82%)
  matrix products  19.6 us (9%)
  between operations  13.4 us (6%)
  starting transfers between devices  4.37 us (2%)
    all_gather x1, waiting for transfers between devices, on_device(): lax.all_gather(queries, 'blk', axis=0, tiled=True)  175 us
    dot_general x1, matrix products, on_device(): lax.dot_general(unit, lax.all_gather(queries, 'blk', axis=0, tiled=True),...  10.8 us
    all_to_all x1, waiting for transfers between devices, on_device(): lax.all_to_all(stacked, 'grp', split_axis=1, concat_axis=2, tiled=True)  10.5 us
    dot_general x2, matrix products, project(): jnp.einsum('lctd,ldr->lctr', rows, matrix, preferred_element_type=jnp.flo...  8.2 us
  transfers between devices with their start and end apart: 2, of which 2 were waited for; matrix products, arithmetic and copies ran while one was open for 4% of the time, Pallas kernels for 0%

commit v1 on v0

--- a/solution.py
+++ b/solution.py
@@ -34,7 +34,9 @@
     unit = (grads * scale).astype(jnp.bfloat16)
     return lax.dot_general(
         unit,
-        lax.all_gather(queries, "blk", axis=0, tiled=True),
+        jnp.concatenate(
+            lax.all_to_all(jnp.stack([queries] * lax.axis_size("blk")), "blk", 0, 0), axis=0
+        ),
         (((1,), (1,)), ((), ())),
         preferred_element_type=jnp.float32,
     )

time: 226 us -> 385 us (1.70)
  the two profiles are of different devices: /device:TPU:0 before, /device:TPU:8 now
where the time goes in v1:
time: 385 us
  waiting for transfers between devices  337 us (88%)
  matrix products  19.8 us (5%)
  blocking collectives  11.6 us (3%)
  starting transfers between devices  8.77 us (2%)
  local copies, waits for them, and re-layouts  7.14 us (2%)
    all_to_all x1, waiting for transfers between devices, on_device(): lax.all_to_all(jnp.stack([queries] * lax.axis_size('blk')), 'blk', 0, 0)  337 us
    all_to_all x1, blocking collectives, on_device(): lax.all_to_all(stacked, 'grp', split_axis=1, concat_axis=2, tiled=True)  11.6 us
    dot_general x1, matrix products, on_device(): lax.dot_general(unit, jnp.concatenate(lax.all_to_all(jnp.stack([queries]...  10.8 us
    all_to_all x1, starting transfers between devices, on_device(): lax.all_to_all(jnp.stack([queries] * lax.axis_size('blk')), 'blk', 0, 0)  8.77 us
    dot_general x2, matrix products, project(): jnp.einsum('lctd,ldr->lctr', rows, matrix, preferred_element_type=jnp.flo...  8.46 us
  transfers between devices with their start and end apart: 1, of which 1 were waited for; matrix products, arithmetic and copies ran while one was open for 0% of the time, Pallas kernels for 0%

profile of v1, /device:TPU:8, one launch (start us, length us, event | category | flops | bytes accessed | tf_op | source)
XLA Modules:
  0.0 384.6 jit_solution(11900119224105218818)
XLA Ops:
  0.0 0.0 copy-start
  0.0 0.0 copy-start.3
  0.0 0.0 copy-start.2
  0.0 1.0 copy-done
  1.0 6.1 %fusion.10 = bf16[1,16,64,64]{3,2,1,0:T(8,128)(2,1)S(1)} fusion(bf16[1,16,64,4096]{3,2,1,0:T(8,128)(2,1)} %param.6, bf16[1,4096,64]{1,2,0:T(8,128)(2,1)S(1)} %copy-done), kind=kOutput, calls=%fused_computation.6 | convolution fusion | flops 536936448 | bytes 9043968 | tf_op jit(solution)/shard_map/lctd,ldr->lctr/dot_general | solution.py:8
  7.2 0.0 copy-done.3
  7.2 0.0 copy-done.2
  7.2 0.0 copy-start.1
  7.2 2.3 fusion.13
  9.5 0.2 maximum_bitcast_fusion
  9.7 11.6 %all_to_all.23 = bf16[1,16,64,128]{3,2,0,1:T(8,128)(2,1)S(1)} all-to-all(bf16[1,16,64,128]{3,2,0,1:T(8,128)(2,1)S(1)} %maximum_bitcast_fusion), channel_id=1, replica_groups=mesh['blk'=32,'grp'=4] {'grp'}, dimensions={1} | all-to-all | bytes 524288 | tf_op jit(solution)/shard_map/all_to_all | solution.py:29
  21.3 0.0 copy-done.1
  21.3 5.9 %stack.2 = bf16[32,64,4096]{2,1,0:T(8,128)(2,1)} broadcast(bf16[64,4096]{1,0:T(8,128)(2,1)S(1)} %copy-done.1), dimensions={1,2} | broadcast | bytes 17301504 | tf_op jit(solution)/shard_map/stack | solution.py:38
  27.2 0.0 copy-start.4
  27.2 8.8 %all-to-all-start.1 = ((bf16[32,64,4096]{2,1,0:T(8,128)(2,1)}), bf16[32,64,4096]{2,1,0:T(8,128)(2,1)}, u32[]{:S(2)}, u32[]{:S(2)}) async-start(bf16[32,64,4096]{2,1,0:T(8,128)(2,1)} %stack.2), calls=%async_computation.1 | async-start | bytes 33554432 | tf_op jit(solution)/shard_map/all_to_all | solution.py:38
  36.0 0.0 copy-done.4
  36.0 0.1 dynamic_slice.3
  36.1 0.1 fusion.22
  36.2 0.6 multiply_reduce_fusion
  36.8 0.1 multiply_convert_fusion
  36.9 0.1 convert_element_type.31
  37.0 336.8 %all-to-all-done.1 = bf16[32,64,4096]{2,1,0:T(8,128)(2,1)} async-done(((bf16[32,64,4096]{2,1,0:T(8,128)(2,1)}), bf16[32,64,4096]{2,1,0:T(8,128)(2,1)}, u32[]{:S(2)}, u32[]{:S(2)}) %all-to-all-start.1) | async-done | bytes 16777248 | tf_op jit(solution)/shard_map/all_to_all | solution.py:38
  373.8 10.8 %fusion.23 = f32[4,2048]{1,0:T(4,128)} fusion(bf16[4,4096]{1,0:T(4,128)(2,1)S(1)} %convert_element_type.31, bf16[2048,4096]{1,0:T(8,128)(2,1)} %bitcast.14), kind=kOutput, calls=%fused_computation.21 | convolution fusion | flops 67108864 | bytes 16842752 | tf_op jit(solution)/shard_map/dot_general | solution.py:35
  (2 shorter events, 0.0 us)
Async XLA Ops:
  0.0 1.0 copy-start
  0.0 7.2 %copy-start.3 = (bf16[1,4096,64]{1,2,0:T(8,128)(2,1)S(1)}, bf16[1,4096,64]{1,2,0:T(8,128)(2,1)}, u32[]{:S(2)}) copy-start(bf16[1,4096,64]{1,2,0:T(8,128)(2,1)} %param.9) | copy-start | bytes 1572868
  0.0 7.2 %copy-start.2 = (bf16[1,16,64,4096]{3,2,1,0:T(8,128)(2,1)S(1)}, bf16[1,16,64,4096]{3,2,1,0:T(8,128)(2,1)}, u32[]{:S(2)}) copy-start(bf16[1,16,64,4096]{3,2,1,0:T(8,128)(2,1)} %param.7) | copy-start | bytes 25165828
  7.2 14.1 %copy-start.1 = (bf16[64,4096]{1,0:T(8,128)(2,1)S(1)}, bf16[64,4096]{1,0:T(8,128)(2,1)}, u32[]{:S(2)}) copy-start(bf16[64,4096]{1,0:T(8,128)(2,1)} %param.11) | copy-start | bytes 1572868
  27.2 8.8 %copy-start.4 = (s32[16]{0:T(128)S(1)}, s32[16]{0:T(128)}, u32[]{:S(2)}) copy-start(s32[16]{0:T(128)} %param.10) | copy-start | bytes 196
  27.2 346.6 %all-to-all-start.1 = ((bf16[32,64,4096]{2,1,0:T(8,128)(2,1)}), bf16[32,64,4096]{2,1,0:T(8,128)(2,1)}, u32[]{:S(2)}, u32[]{:S(2)}) async-start(bf16[32,64,4096]{2,1,0:T(8,128)(2,1)} %stack.2), calls=%async_computation.1 | async-start | bytes 33554432 | tf_op jit(solution)/shard_map/all_to_all | solution.py:38
